TPU v7x, 32 devices: a whole 2x2x4 slice. The times are simulated.
32 devices in a mesh: fibre: 2 (over y), chan: 4 (over z), win: 2 (over x), grp: 2 (over core).
Axes of the slice: x: 2, y: 2, z: 4, core: 2. Of those that a mesh axis runs over, the one named last changes fastest.
Arguments:
- file_rows: bfloat16 [1280, 8192], P(('fibre', 'chan'), 'win'), parts along dimension 0, may hold values from -150 to 150
- channel_list: int32 [1280], P(('fibre', 'chan')), parts along dimension 0, may hold values from 0 to 512, as said below
- filter_taps: bfloat16 [64], replicated, may hold values from -0.75 to 0.75
- source_channels: int32 [8, 64], P(('fibre', 'grp')), parts along dimension 0, may hold values from 0 to 511, as said below
Outputs:
- correlations: float32 [1024, 256, 256], P(('fibre', 'chan', 'win'), 'grp'), parts along dimension 0
There are 2 independent parts, one for each index of `fibre`. A program takes and returns all parts, laid end to end along the dimension named above; an argument that names none is the same for every part. Nothing has to cross between parts.
Inputs may be any that keep to these rules, and one draw needn't show every extreme that they name: `channel_list`: the rows of one device are the 160 consecutive rows d * 160 on; its rows that hold data come first. Every channel appears exactly once over all devices; of one device's rows at most 32 lie in one block of channels b * 128 to (b + 1) * 128 - 1, and some device reaches 32 in every block; every device has rows without data. `source_channels`: all 256 channels are different.
All inputs are finite; a program needn't handle non-finite values.
Results may differ from a plain program's by a relative error of at most 0.0076.
Values may be sent and summed in bfloat16 or wider, within the bound.
A program may use at most 128 MiB of HBM per device.

v0:
```python
import functools
import math

import jax
import jax.numpy as jnp
import ml_dtypes
import numpy as np
from jax import lax
from jax.experimental import pallas as pl
from jax.experimental.pallas import tpu as pltpu
from jax.sharding import PartitionSpec as P

L = 4096
FB = 256
F0 = 8
LAGS = 256
TAPS = 64
HALF = 64
SMOOTH = 8
CH_DEV = 128
SEG = 64
CHUNK = 256
TAIL = 16
VMEM_LIMIT = 60 * 1024 * 1024

epsilon = 1e-06
water_level = 0.1


def phase_tables():
    bins = np.arange(FB) + F0
    digits = np.arange(SEG)
    coarse = np.mod(digits[:, None] * SEG * bins[None, :], L) * (2.0 * math.pi / L)
    fine = np.mod(digits[:, None] * bins[None, :], L) * (2.0 * math.pi / L)
    pair = lambda angle: np.concatenate([np.cos(angle), np.sin(angle)], axis=1).astype(np.float32)
    shifts = np.arange(LAGS) - LAGS // 2
    turn = np.mod(bins[:, None] * shifts[None, :], L).astype(np.float32) * np.float32(2.0 * math.pi / L)
    inverse = np.concatenate([np.cos(turn), -np.sin(turn)], axis=0) / math.sqrt(FB)
    return pair(coarse), pair(fine), inverse.astype(ml_dtypes.bfloat16)


def dot(a, b):
    return jnp.dot(a, b, preferred_element_type=jnp.float32)


def iota(shape, axis):
    return lax.broadcasted_iota(jnp.int32, shape, axis)


def whiten_kernel(taps_ref, coarse_ref, fine_ref, labels_ref, rows_ref, out_ref,
                  table, filt, size, normed, toeplitz):
    count = rows_ref.shape[0]

    moved = jnp.broadcast_to(taps_ref[...], (128, 256))
    row = iota((128, 256), 0)
    for bit in range(7):
        moved = jnp.where((row >> bit) & 1 == 1, pltpu.roll(moved, 2**bit, 1), moved)
    moved = moved.astype(jnp.bfloat16)
    here, before = moved[:, :128], moved[:, 128:]
    zero = jnp.zeros((128, 128), jnp.bfloat16)
    toeplitz[0:128, :] = jnp.concatenate([before, zero], axis=1)
    toeplitz[128:256, :] = jnp.concatenate([here, before], axis=1)
    toeplitz[256:384, :] = jnp.concatenate([zero, here], axis=1)

    for start in range(0, L, CHUNK):
        if start == 0:
            part = dot(rows_ref[:, 0:CHUNK], toeplitz[128:384, :])
        else:
            part = dot(rows_ref[:, start - 128 : start + CHUNK], toeplitz[...])
        filt[:, start : start + CHUNK] = part
        size[:, start : start + CHUNK] = jnp.abs(part).astype(jnp.bfloat16)

    def fill(a, carry):
        ca = coarse_ref[pl.ds(a, 1), :FB]
        sa = coarse_ref[pl.ds(a, 1), FB:]
        cb = fine_ref[:, :FB]
        sb = fine_ref[:, FB:]
        where = pl.ds(pl.multiple_of(a * SEG, SEG), SEG)
        table[where, :FB] = (ca * cb - sa * sb).astype(jnp.bfloat16)
        table[where, FB:] = (-(sa * cb + ca * sb)).astype(jnp.bfloat16)
        return carry

    lax.fori_loop(0, L // SEG, fill, 0)

    reach = jnp.abs(iota((512, CHUNK), 0) - 128 - iota((512, CHUNK), 1)) <= HALF
    band = reach.astype(jnp.float32).astype(jnp.bfloat16)
    for start in range(0, L, CHUNK):
        low, high = max(start - 128, 0), min(start + CHUNK + 128, L)
        first = low - (start - 128)
        total = dot(size[:, low:high], band[first : first + high - low])
        position = start + iota((1, CHUNK), 1)
        width = jnp.minimum(position, HALF) + jnp.minimum(L - 1 - position, HALF) + 1
        scale = 1.0 / width.astype(jnp.float32)
        normed[:, start : start + CHUNK] = (
            filt[:, start : start + CHUNK] / (total * scale + epsilon)
        ).astype(jnp.bfloat16)

    spectrum = dot(normed[...], table[...])
    real, imag = spectrum[:, :FB], spectrum[:, FB:]
    energy = real * real + imag * imag
    near = (jnp.abs(iota((FB, FB), 0) - iota((FB, FB), 1)) <= SMOOTH)
    near = near.astype(jnp.float32).astype(jnp.bfloat16)
    upper = energy.astype(jnp.bfloat16)
    left = energy - upper.astype(jnp.float32)
    middle = left.astype(jnp.bfloat16)
    lower = (left - middle.astype(jnp.float32)).astype(jnp.bfloat16)
    total = dot(upper, near) + dot(middle, near) + dot(lower, near)
    k = iota((1, FB), 1)
    width = jnp.minimum(k, SMOOTH) + jnp.minimum(FB - 1 - k, SMOOTH) + 1
    smooth = total / width.astype(jnp.float32)
    level = jnp.sum(energy, axis=1, keepdims=True) * (1.0 / FB)
    factor = lax.rsqrt(smooth + water_level * level + epsilon)
    out_ref[0:count, :FB] = (real * factor).astype(jnp.bfloat16)
    out_ref[0:count, FB:] = (imag * factor).astype(jnp.bfloat16)

    labels = labels_ref[...]
    place = iota((TAIL, 2 * FB), 0)
    digits = jnp.where(place == 0, labels >> 6, jnp.where(place == 1, labels & 63, 0))
    out_ref[count : count + TAIL, :] = digits.astype(jnp.float32).astype(jnp.bfloat16)


def select_kernel(wins, sources_ref, spectra_ref, chan_ref, src_ref):
    blocks = spectra_ref.shape[0]
    count = spectra_ref.shape[1] - TAIL
    channels = chan_ref.shape[0]
    groups, width = sources_ref.shape
    first = lax.axis_index("chan") * CH_DEV + lax.axis_index("win") * channels
    diagonal = iota((width, width), 0) == iota((width, width), 1)
    wanted = [
        jnp.sum(jnp.where(diagonal, sources_ref[g : g + 1, :], 0), axis=1, keepdims=True)
        for g in range(groups)
    ]
    wanted.append(first + iota((channels, 1), 0))
    wanted = jnp.concatenate(wanted, axis=0)
    total = None
    for block in range(blocks):
        digits = spectra_ref[block, count : count + TAIL, :count].astype(jnp.float32)
        labels = (digits[0:1, :] * 64.0 + digits[1:2, :]).astype(jnp.int32)
        pick = (wanted == labels).astype(jnp.float32).astype(jnp.bfloat16)
        part = dot(pick, spectra_ref[block, :count, :])
        total = part if total is None else total + part
    src_ref[...] = total[: groups * width]
    chan_ref[...] = total[groups * width :]


def correlate_kernel(wins, inverse_ref, src_ref, chan_ref, out_ref):
    inverse = inverse_ref[...]
    for c in range(out_ref.shape[0]):
        real = imag = None
        for w in range(wins):
            at = w * 2 * FB
            p, q = src_ref[:, at : at + FB], src_ref[:, at + FB : at + 2 * FB]
            a, b = chan_ref[c : c + 1, at : at + FB], chan_ref[c : c + 1, at + FB : at + 2 * FB]
            re, im = a * p + b * q, b * p - a * q
            real = re if real is None else real + re
            imag = im if imag is None else imag + im
        cross = jnp.concatenate([real.astype(jnp.bfloat16), imag.astype(jnp.bfloat16)], axis=1)
        out_ref[c] = dot(cross, inverse)


def local(file_rows, channel_list, filter_taps, source_channels):
    chan_count = lax.axis_size("chan")
    wins = lax.axis_size("win")
    count = chan_count * (CH_DEV // 4)
    channels = CH_DEV // wins
    groups, width = source_channels.shape
    sources = groups * width
    assert file_rows.shape[1] == L and count <= 2 * FB
    coarse, fine, inverse = phase_tables()

    taps = jnp.pad(filter_taps.astype(jnp.float32), (0, 256 - TAPS)).reshape(1, 256)
    labels = jnp.pad(
        channel_list[:count], (0, 2 * FB - count), constant_values=chan_count * CH_DEV
    ).reshape(1, 2 * FB)

    whole = lambda shape: pl.BlockSpec(shape, lambda i: (0,) * len(shape))
    mine = pl.pallas_call(
        whiten_kernel,
        grid=(1,),
        in_specs=[
            whole((1, 256)),
            whole((SEG, 2 * FB)),
            whole((SEG, 2 * FB)),
            whole((1, 2 * FB)),
            whole((count, L)),
        ],
        out_specs=whole((count + TAIL, 2 * FB)),
        out_shape=jax.ShapeDtypeStruct((count + TAIL, 2 * FB), jnp.bfloat16),
        scratch_shapes=[
            pltpu.VMEM((L, 2 * FB), jnp.bfloat16),
            pltpu.VMEM((count, L), jnp.float32),
            pltpu.VMEM((count, L), jnp.bfloat16),
            pltpu.VMEM((count, L), jnp.bfloat16),
            pltpu.VMEM((384, 256), jnp.bfloat16),
        ],
        compiler_params=pltpu.CompilerParams(vmem_limit_bytes=VMEM_LIMIT),
        name="whiten",
    )(taps, jnp.asarray(coarse), jnp.asarray(fine), labels, file_rows)

    spectra = lax.all_gather(mine, ("chan", "win"), axis=0, tiled=False)
    spectra = spectra.reshape(chan_count, wins, count + TAIL, 2 * FB)

    chan_spec, src_spec = pl.pallas_call(
        functools.partial(select_kernel, wins),
        grid=(wins,),
        in_specs=[
            whole((groups, width)),
            pl.BlockSpec((chan_count, None, count + TAIL, 2 * FB), lambda w: (0, w, 0, 0)),
        ],
        out_specs=[
            pl.BlockSpec((channels, 2 * FB), lambda w: (0, w)),
            pl.BlockSpec((sources, 2 * FB), lambda w: (0, w)),
        ],
        out_shape=[
            jax.ShapeDtypeStruct((channels, wins * 2 * FB), jnp.float32),
            jax.ShapeDtypeStruct((sources, wins * 2 * FB), jnp.float32),
        ],
        compiler_params=pltpu.CompilerParams(vmem_limit_bytes=VMEM_LIMIT),
        name="select",
    )(source_channels, spectra)

    step = 8
    return pl.pallas_call(
        functools.partial(correlate_kernel, wins),
        grid=(channels // step,),
        in_specs=[
            whole((2 * FB, LAGS)),
            whole((sources, wins * 2 * FB)),
            pl.BlockSpec((step, wins * 2 * FB), lambda i: (i, 0)),
        ],
        out_specs=pl.BlockSpec((step, sources, LAGS), lambda i: (i, 0, 0)),
        out_shape=jax.ShapeDtypeStruct((channels, sources, LAGS), jnp.float32),
        compiler_params=pltpu.CompilerParams(vmem_limit_bytes=VMEM_LIMIT),
        name="correlate",
    )(jnp.asarray(inverse), src_spec, chan_spec)


def solution(mesh):
    placed = (P(("fibre", "chan"), "win"), P(("fibre", "chan")), P(), P(("fibre", "grp"), None))
    return jax.shard_map(
        local,
        mesh=mesh,
        in_specs=placed,
        out_specs=P(("fibre", "chan", "win"), "grp", None),
        check_vma=False,
    )
```

profile of v0, /device:TPU:0, one launch (start us, length us, event | category | flops | bytes accessed | tf_op | source)
XLA Modules:
  0.0 77.5 jit_solution(541779019087669469)
XLA Ops:
  6.5 0.0 all-gather.3.cloned.1.call-start
  6.5 0.7 slice.3
  7.2 1.2 %pad_convert_fusion = f32[256]{0:T(256)} fusion(bf16[64]{0:T(256)(128)(2,1)} %param.9), kind=kLoop, calls=%fused_computation | loop fusion | flops 256 | bytes 1152 | tf_op jit(solution)/shard_map/reshape | solution.py:171
  8.4 0.6 pad.10
  9.0 6.3 %whiten.1 = bf16[144,512]{1,0:T(8,128)(2,1)} custom-call(f32[1,256]{1,0:T(1,128)} %bitcast.5, f32[64,512]{1,0:T(8,128)} %constant.12.clone.coarse_ref, f32[64,512]{1,0:T(8,128)} %constant.13.clone.fine_ref, s32[1,512]{1,0:T(1,128)} %bitcast.4, bf16[160,4096]{1,0:T(8,128)(2,1)} %rows_ref.1), custom_call_target="tpu_custom_call" | custom-call | tf_op jit(solution)/shard_map/whiten/pallas_call | solution.py:177
  15.3 0.0 all-gather.3.cloned.1.call-update
  15.3 44.0 %all-gather.3.cloned.1.call-done = bf16[1152,512]{1,0:T(8,128)(2,1)} async-done(((bf16[144,512]{1,0:T(8,128)(2,1)}), bf16[1152,512]{1,0:T(8,128)(2,1)}) %all-gather.3.cloned.1.call-update) | async-done | bytes 1179664 | tf_op jit(solution)/shard_map/all_gather | solution.py:200
  59.3 2.9 %select.3 = (f32[64,1024]{1,0:T(8,128)}, f32[128,1024]{1,0:T(8,128)}) custom-call(s32[2,64]{1,0:T(2,128)} %sources_ref.1, bf16[4,2,144,512]{3,2,1,0:T(8,128)(2,1)} %bitcast.3), custom_call_target="tpu_custom_call" | custom-call | tf_op jit(solution)/shard_map/select/pallas_call | solution.py:203
  62.2 8.5 %correlate.1 = f32[64,128,256]{2,1,0:T(8,128)} custom-call(bf16[512,256]{1,0:T(8,128)(2,1)} %constant.14.clone.inverse_ref, f32[128,1024]{1,0:T(8,128)} %get-tuple-element.7.src_ref, f32[64,1024]{1,0:T(8,128)} %get-tuple-element.8.chan_ref), custom_call_target="tpu_custom_call" | custom-call | tf_op jit(solution)/shard_map/correlate/pallas_call | solution.py:223
Async XLA Ops:
  6.5 52.8 %all-gather.3.cloned.1.call-start = ((), (), s32[]{:S(2)}) async-start(), calls=%async_computation | async-start | bytes 1327104 | tf_op jit(solution)/shard_map/all_gather | solution.py:200
Sparse Core Ops, SparseCore 0:
  15.4 43.8 all-gather.2
where the time goes:
time: 78 us; the launch traced here: 77.5 us
  waiting for transfers between devices  44 us (56%)
  Pallas kernels  17.6 us (23%)
  between operations  13.4 us (17%)
  local copies, waits for them, and re-layouts  1.25 us (2%)
  other arithmetic  1.2 us (2%)
    all_gather x1, waiting for transfers between devices, local(): spectra = lax.all_gather(mine, ('chan', 'win'), axis=0, tiled=False)  44 us
    pallas_call x1, Pallas kernels, local(): pl.pallas_call(functools.partial(correlate_kernel, wins), grid=(channels...  8.48 us
    pallas_call x1, Pallas kernels, local(): pl.pallas_call(whiten_kernel, grid=(1,), in_specs=[whole((1, 256)), whole...  6.31 us
    pallas_call x1, Pallas kernels, local(): pl.pallas_call(functools.partial(select_kernel, wins), grid=(wins,), in_s...  2.85 us
  transfers between devices with their start and end apart: 1, of which 1 were waited for; matrix products, arithmetic and copies ran while one was open for 0% of the time, Pallas kernels for 0%

commit v1 on v0

--- a/solution.py
+++ b/solution.py
@@ -47,11 +47,30 @@
     return lax.broadcasted_iota(jnp.int32, shape, axis)
 
 
-def whiten_kernel(taps_ref, coarse_ref, fine_ref, labels_ref, rows_ref, out_ref,
-                  table, filt, size, normed, toeplitz):
+def whiten_kernel(taps_ref, coarse_ref, fine_ref, labels_ref, file_ref, out_ref,
+                  rows_ref, table, filt, size, normed, toeplitz, wide_taps, wide_labels, sem):
     count = rows_ref.shape[0]
-
-    moved = jnp.broadcast_to(taps_ref[...], (128, 256))
+    total_count = count * lax.axis_size("grp")
+
+    begin = pl.multiple_of(lax.axis_index("grp") * count, count)
+    fetch = pltpu.make_async_copy(file_ref.at[pl.ds(begin, count), :], rows_ref, sem)
+    fetch.start()
+
+    def fill(a, carry):
+        ca = coarse_ref[pl.ds(a, 1), :FB]
+        sa = coarse_ref[pl.ds(a, 1), FB:]
+        cb = fine_ref[:, :FB]
+        sb = fine_ref[:, FB:]
+        where = pl.ds(pl.multiple_of(a * SEG, SEG), SEG)
+        table[where, :FB] = (ca * cb - sa * sb).astype(jnp.bfloat16)
+        table[where, FB:] = (-(sa * cb + ca * sb)).astype(jnp.bfloat16)
+        return carry
+
+    lax.fori_loop(0, L // SEG, fill, 0)
+
+    wide_taps[...] = jnp.zeros_like(wide_taps)
+    wide_taps[:, :TAPS] = taps_ref[...].astype(jnp.float32)
+    moved = jnp.broadcast_to(wide_taps[...], (128, 256))
     row = iota((128, 256), 0)
     for bit in range(7):
         moved = jnp.where((row >> bit) & 1 == 1, pltpu.roll(moved, 2**bit, 1), moved)
@@ -62,6 +81,7 @@
     toeplitz[128:256, :] = jnp.concatenate([here, before], axis=1)
     toeplitz[256:384, :] = jnp.concatenate([zero, here], axis=1)
 
+    fetch.wait()
     for start in range(0, L, CHUNK):
         if start == 0:
             part = dot(rows_ref[:, 0:CHUNK], toeplitz[128:384, :])
@@ -69,18 +89,6 @@
             part = dot(rows_ref[:, start - 128 : start + CHUNK], toeplitz[...])
         filt[:, start : start + CHUNK] = part
         size[:, start : start + CHUNK] = jnp.abs(part).astype(jnp.bfloat16)
-
-    def fill(a, carry):
-        ca = coarse_ref[pl.ds(a, 1), :FB]
-        sa = coarse_ref[pl.ds(a, 1), FB:]
-        cb = fine_ref[:, :FB]
-        sb = fine_ref[:, FB:]
-        where = pl.ds(pl.multiple_of(a * SEG, SEG), SEG)
-        table[where, :FB] = (ca * cb - sa * sb).astype(jnp.bfloat16)
-        table[where, FB:] = (-(sa * cb + ca * sb)).astype(jnp.bfloat16)
-        return carry
-
-    lax.fori_loop(0, L // SEG, fill, 0)
 
     reach = jnp.abs(iota((512, CHUNK), 0) - 128 - iota((512, CHUNK), 1)) <= HALF
     band = reach.astype(jnp.float32).astype(jnp.bfloat16)
@@ -113,15 +121,88 @@
     out_ref[0:count, :FB] = (real * factor).astype(jnp.bfloat16)
     out_ref[0:count, FB:] = (imag * factor).astype(jnp.bfloat16)
 
-    labels = labels_ref[...]
+    wide_labels[...] = jnp.zeros_like(wide_labels)
+    wide_labels[:, :total_count] = labels_ref[:, :total_count]
+    labels = wide_labels[...]
     place = iota((TAIL, 2 * FB), 0)
     digits = jnp.where(place == 0, labels >> 6, jnp.where(place == 1, labels & 63, 0))
     out_ref[count : count + TAIL, :] = digits.astype(jnp.float32).astype(jnp.bfloat16)
 
 
+def other(index, step):
+    for bit in range(step.bit_length()):
+        if (step >> bit) & 1:
+            index = index + 2**bit - 2 ** (bit + 1) * ((index // 2**bit) % 2)
+    return index
+
+
+def gather_kernel(sizes, mine_ref, out_ref, own_sem, z_sems, x_sems, c_sems):
+    zs, xs, cs = sizes
+    z, x, c = lax.axis_index("chan"), lax.axis_index("win"), lax.axis_index("grp")
+
+    barrier = pltpu.get_barrier_semaphore()
+    for axis, size, index in (("chan", zs, z), ("win", xs, x), ("grp", cs, c)):
+        for step in range(1, size):
+            pl.semaphore_signal(
+                barrier, inc=1, device_id={axis: other(index, step)},
+                device_id_type=pl.DeviceIdType.MESH,
+            )
+    pl.semaphore_wait(barrier, zs + xs + cs - 3)
+
+    def send(source, slot, sems, at, axis, target):
+        copy = pltpu.make_async_remote_copy(
+            src_ref=source,
+            dst_ref=out_ref.at[slot],
+            send_sem=sems.at[(0, *at)],
+            recv_sem=sems.at[(1, *at)],
+            device_id={axis: target},
+            device_id_type=pl.DeviceIdType.MESH,
+        )
+        copy.start()
+        return copy
+
+    def pass_on(source, slot, d, copies):
+        for e in range(1, xs):
+            copies[d, e] = send(source, slot, x_sems, (d, e), "win", other(x, e))
+
+    def share(source, slot, d, e, copies):
+        for f in range(1, cs):
+            copies[d, e, f] = send(source, slot, c_sems, (d, e, f), "grp", other(c, f))
+
+    own = (z, x, c)
+    along_z, along_x, along_c = {}, {}, {}
+    pass_on(mine_ref, own, 0, along_x)
+    for d in range(1, zs):
+        along_z[d] = send(mine_ref, own, z_sems, (d,), "chan", other(z, d))
+    share(mine_ref, own, 0, 0, along_c)
+    keep = pltpu.make_async_copy(mine_ref, out_ref.at[own], own_sem)
+    keep.start()
+
+    def relay_x(d):
+        for e in range(1, xs):
+            along_x[d, e].wait_recv()
+            slot = (other(z, d), other(x, e), c)
+            share(out_ref.at[slot], slot, d, e, along_c)
+
+    for d in range(1, zs):
+        along_z[d].wait_recv()
+        slot = (other(z, d), x, c)
+        pass_on(out_ref.at[slot], slot, d, along_x)
+        share(out_ref.at[slot], slot, d, 0, along_c)
+    for d in range(zs):
+        relay_x(d)
+    for copy in along_c.values():
+        copy.wait_recv()
+    for copies in (along_z, along_x, along_c):
+        for copy in copies.values():
+            copy.wait_send()
+    keep.wait()
+
+
 def select_kernel(wins, sources_ref, spectra_ref, chan_ref, src_ref):
     blocks = spectra_ref.shape[0]
-    count = spectra_ref.shape[1] - TAIL
+    cores = spectra_ref.shape[1]
+    count = spectra_ref.shape[2] - TAIL
     channels = chan_ref.shape[0]
     groups, width = sources_ref.shape
     first = lax.axis_index("chan") * CH_DEV + lax.axis_index("win") * channels
@@ -134,10 +215,11 @@
     wanted = jnp.concatenate(wanted, axis=0)
     total = None
     for block in range(blocks):
-        digits = spectra_ref[block, count : count + TAIL, :count].astype(jnp.float32)
+        digits = spectra_ref[block, 0, count : count + TAIL, : cores * count].astype(jnp.float32)
         labels = (digits[0:1, :] * 64.0 + digits[1:2, :]).astype(jnp.int32)
         pick = (wanted == labels).astype(jnp.float32).astype(jnp.bfloat16)
-        part = dot(pick, spectra_ref[block, :count, :])
+        rows = jnp.concatenate([spectra_ref[block, c, :count, :] for c in range(cores)], axis=0)
+        part = dot(pick, rows)
         total = part if total is None else total + part
     src_ref[...] = total[: groups * width]
     chan_ref[...] = total[groups * width :]
@@ -168,44 +250,66 @@
     assert file_rows.shape[1] == L and count <= 2 * FB
     coarse, fine, inverse = phase_tables()
 
-    taps = jnp.pad(filter_taps.astype(jnp.float32), (0, 256 - TAPS)).reshape(1, 256)
-    labels = jnp.pad(
-        channel_list[:count], (0, 2 * FB - count), constant_values=chan_count * CH_DEV
-    ).reshape(1, 2 * FB)
-
+    cores = lax.axis_size("grp")
+    share = count // cores
     whole = lambda shape: pl.BlockSpec(shape, lambda i: (0,) * len(shape))
     mine = pl.pallas_call(
         whiten_kernel,
         grid=(1,),
         in_specs=[
-            whole((1, 256)),
+            whole((1, TAPS)),
             whole((SEG, 2 * FB)),
             whole((SEG, 2 * FB)),
-            whole((1, 2 * FB)),
-            whole((count, L)),
-        ],
-        out_specs=whole((count + TAIL, 2 * FB)),
-        out_shape=jax.ShapeDtypeStruct((count + TAIL, 2 * FB), jnp.bfloat16),
+            whole((1, channel_list.shape[0])),
+            pl.BlockSpec(memory_space=pl.ANY),
+        ],
+        out_specs=whole((share + TAIL, 2 * FB)),
+        out_shape=jax.ShapeDtypeStruct((share + TAIL, 2 * FB), jnp.bfloat16),
         scratch_shapes=[
+            pltpu.VMEM((share, L), jnp.bfloat16),
             pltpu.VMEM((L, 2 * FB), jnp.bfloat16),
-            pltpu.VMEM((count, L), jnp.float32),
-            pltpu.VMEM((count, L), jnp.bfloat16),
-            pltpu.VMEM((count, L), jnp.bfloat16),
+            pltpu.VMEM((share, L), jnp.float32),
+            pltpu.VMEM((share, L), jnp.bfloat16),
+            pltpu.VMEM((share, L), jnp.bfloat16),
             pltpu.VMEM((384, 256), jnp.bfloat16),
+            pltpu.VMEM((1, 256), jnp.float32),
+            pltpu.VMEM((1, 2 * FB), jnp.int32),
+            pltpu.SemaphoreType.DMA,
         ],
         compiler_params=pltpu.CompilerParams(vmem_limit_bytes=VMEM_LIMIT),
         name="whiten",
-    )(taps, jnp.asarray(coarse), jnp.asarray(fine), labels, file_rows)
-
-    spectra = lax.all_gather(mine, ("chan", "win"), axis=0, tiled=False)
-    spectra = spectra.reshape(chan_count, wins, count + TAIL, 2 * FB)
+    )(
+        filter_taps.reshape(1, TAPS),
+        jnp.asarray(coarse),
+        jnp.asarray(fine),
+        channel_list.reshape(1, -1),
+        file_rows,
+    )
+
+    block = (share + TAIL, 2 * FB)
+    gathered = (chan_count, wins, cores, *block)
+    small = math.prod(gathered) * 2 <= 8 * 1024 * 1024
+    spectra = pl.pallas_call(
+        functools.partial(gather_kernel, (chan_count, wins, cores)),
+        in_specs=[pl.BlockSpec(memory_space=pltpu.VMEM)],
+        out_specs=pl.BlockSpec(memory_space=pltpu.VMEM if small else pl.ANY),
+        out_shape=jax.ShapeDtypeStruct(gathered, jnp.bfloat16),
+        scratch_shapes=[
+            pltpu.SemaphoreType.DMA,
+            pltpu.SemaphoreType.DMA((2, chan_count)),
+            pltpu.SemaphoreType.DMA((2, chan_count, wins)),
+            pltpu.SemaphoreType.DMA((2, chan_count, wins, cores)),
+        ],
+        compiler_params=pltpu.CompilerParams(collective_id=0, has_side_effects=True),
+        name="gather",
+    )(mine)
 
     chan_spec, src_spec = pl.pallas_call(
         functools.partial(select_kernel, wins),
         grid=(wins,),
         in_specs=[
             whole((groups, width)),
-            pl.BlockSpec((chan_count, None, count + TAIL, 2 * FB), lambda w: (0, w, 0, 0)),
+            pl.BlockSpec((chan_count, None, cores, *block), lambda w: (0, w, 0, 0, 0)),
         ],
         out_specs=[
             pl.BlockSpec((channels, 2 * FB), lambda w: (0, w)),

time: 78 us -> 38 us (0.49)
  waiting for transfers between devices: 44 us -> 0 us
  Pallas kernels: 17.6 us -> 37.4 us
  between operations: 13.4 us -> 0.02 us
  local copies, waits for them, and re-layouts: 1.25 us -> 0 us
  other arithmetic: 1.2 us -> 0 us
    all_gather x1 -> x0, waiting for transfers between devices: 44 us -> none  [local(): spectra = lax.all_gather(mine, ('chan', 'win'), axis=0, tiled=False)]
    pallas_call x1 -> x2, Pallas kernels: 6.31 us -> 26 us  [the longest x1 20.4 us: local(): pl.pallas_call(functools.partial(gather_kernel, (chan_count, wins, cores)...]
    reshape x1 -> x0, other arithmetic: 1.2 us -> none  [local(): jnp.pad(filter_taps.astype(jnp.float32), (0, 256 - TAPS)).reshape(1, 256)]
  transfers between devices with their start and end apart: 1 -> 0, of which waited for: 1 -> 0; matrix products, arithmetic and copies ran while one was open for 0% -> 0% of each run, Pallas kernels for 0% -> 0%
where the time goes in v1:
time: 38 us; the launch traced here: 37.4 us
  Pallas kernels  37.4 us (98%)
    pallas_call x1, Pallas kernels, local(): pl.pallas_call(functools.partial(gather_kernel, (chan_count, wins, cores)...  20.4 us
    pallas_call x1, Pallas kernels, local(): pl.pallas_call(functools.partial(correlate_kernel, wins), grid=(channels...  8.48 us
    pallas_call x1, Pallas kernels, local(): pl.pallas_call(whiten_kernel, grid=(1,), in_specs=[whole((1, TAPS)), whol...  5.66 us
    pallas_call x1, Pallas kernels, local(): pl.pallas_call(functools.partial(select_kernel, wins), grid=(wins,), in_s...  2.89 us

profile of v1, /device:TPU:0, one launch (start us, length us, event | category | flops | bytes accessed | tf_op | source)
XLA Modules:
  0.0 37.4 jit_solution(1658033734473515550)
XLA Ops:
  0.0 5.7 %whiten.1.mine_ref = bf16[80,512]{1,0:T(8,128)(2,1)} custom-call(bf16[1,64]{1,0:T(2,128)(2,1)} %bitcast.3, f32[64,512]{1,0:T(8,128)} %constant.6.clone.coarse_ref, f32[64,512]{1,0:T(8,128)} %constant.7.clone.fine_ref, s32[1,160]{1,0:T(1,128)} %bitcast.2, bf16[160,4096]{1,0:T(8,128)(2,1)} %file_ref.1), custom_call_target="tpu_custom_call" | custom-call | tf_op jit(solution)/shard_map/whiten/pallas_call | solution.py:256
  5.7 20.4 %gather.1.spectra_ref = bf16[4,2,2,80,512]{4,3,2,1,0:T(8,128)(2,1)} custom-call(bf16[80,512]{1,0:T(8,128)(2,1)} %whiten.1.mine_ref), custom_call_target="tpu_custom_call" | custom-call | tf_op jit(solution)/shard_map/gather/pallas_call | solution.py:292
  26.1 2.9 %select.1 = (f32[64,1024]{1,0:T(8,128)}, f32[128,1024]{1,0:T(8,128)}) custom-call(s32[2,64]{1,0:T(2,128)} %sources_ref.1, bf16[4,2,2,80,512]{4,3,2,1,0:T(8,128)(2,1)} %gather.1.spectra_ref), custom_call_target="tpu_custom_call" | custom-call | tf_op jit(solution)/shard_map/select/pallas_call | solution.py:307
  29.0 8.5 %correlate.1 = f32[64,128,256]{2,1,0:T(8,128)} custom-call(bf16[512,256]{1,0:T(8,128)(2,1)} %constant.8.clone.inverse_ref, f32[128,1024]{1,0:T(8,128)} %get-tuple-element.7.src_ref, f32[64,1024]{1,0:T(8,128)} %get-tuple-element.8.chan_ref), custom_call_target="tpu_custom_call" | custom-call | tf_op jit(solution)/shard_map/correlate/pallas_call | solution.py:327

commit v2 on v1

--- a/solution.py
+++ b/solution.py
@@ -19,8 +19,8 @@
 SMOOTH = 8
 CH_DEV = 128
 SEG = 64
+FOLD = 4
 CHUNK = 256
-TAIL = 16
 VMEM_LIMIT = 60 * 1024 * 1024
 
 epsilon = 1e-06
@@ -47,8 +47,8 @@
     return lax.broadcasted_iota(jnp.int32, shape, axis)
 
 
-def whiten_kernel(taps_ref, coarse_ref, fine_ref, labels_ref, file_ref, out_ref,
-                  rows_ref, table, filt, size, normed, toeplitz, wide_taps, wide_labels, sem):
+def whiten_kernel(taps_ref, coarse_ref, fine_ref, labels_ref, file_ref, out_ref, seen_ref,
+                  rows_ref, table, filt, size, normed, toeplitz, wide_taps, sem):
     count = rows_ref.shape[0]
     total_count = count * lax.axis_size("grp")
 
@@ -66,7 +66,7 @@
         table[where, FB:] = (-(sa * cb + ca * sb)).astype(jnp.bfloat16)
         return carry
 
-    lax.fori_loop(0, L // SEG, fill, 0)
+    lax.fori_loop(0, L // FOLD // SEG, fill, 0)
 
     wide_taps[...] = jnp.zeros_like(wide_taps)
     wide_taps[:, :TAPS] = taps_ref[...].astype(jnp.float32)
@@ -99,12 +99,22 @@
         position = start + iota((1, CHUNK), 1)
         width = jnp.minimum(position, HALF) + jnp.minimum(L - 1 - position, HALF) + 1
         scale = 1.0 / width.astype(jnp.float32)
-        normed[:, start : start + CHUNK] = (
+        fold, at = divmod(start, L // FOLD)
+        normed[fold * count : (fold + 1) * count, at : at + CHUNK] = (
             filt[:, start : start + CHUNK] / (total * scale + epsilon)
         ).astype(jnp.bfloat16)
 
-    spectrum = dot(normed[...], table[...])
-    real, imag = spectrum[:, :FB], spectrum[:, FB:]
+    quarters = dot(normed[...], table[...])
+    k = iota((1, FB), 1) + F0
+    real = imag = jnp.zeros((count, FB), jnp.float32)
+    for fold in range(FOLD):
+        turns = (k * fold) % 4
+        cosine = jnp.where(turns == 0, 1.0, jnp.where(turns == 2, -1.0, 0.0))
+        sine = jnp.where(turns == 1, 1.0, jnp.where(turns == 3, -1.0, 0.0))
+        re = quarters[fold * count : (fold + 1) * count, :FB]
+        im = quarters[fold * count : (fold + 1) * count, FB:]
+        real = real + cosine * re + sine * im
+        imag = imag + cosine * im - sine * re
     energy = real * real + imag * imag
     near = (jnp.abs(iota((FB, FB), 0) - iota((FB, FB), 1)) <= SMOOTH)
     near = near.astype(jnp.float32).astype(jnp.bfloat16)
@@ -121,12 +131,8 @@
     out_ref[0:count, :FB] = (real * factor).astype(jnp.bfloat16)
     out_ref[0:count, FB:] = (imag * factor).astype(jnp.bfloat16)
 
-    wide_labels[...] = jnp.zeros_like(wide_labels)
-    wide_labels[:, :total_count] = labels_ref[:, :total_count]
-    labels = wide_labels[...]
-    place = iota((TAIL, 2 * FB), 0)
-    digits = jnp.where(place == 0, labels >> 6, jnp.where(place == 1, labels & 63, 0))
-    out_ref[count : count + TAIL, :] = digits.astype(jnp.float32).astype(jnp.bfloat16)
+    seen_ref[...] = jnp.zeros_like(seen_ref)
+    seen_ref[:, :total_count] = labels_ref[:, :total_count]
 
 
 def other(index, step):
@@ -136,7 +142,8 @@
     return index
 
 
-def gather_kernel(sizes, mine_ref, out_ref, own_sem, z_sems, x_sems, c_sems):
+def gather_kernel(sizes, mine_ref, seen_ref, out_ref, labels_ref,
+                  own_sems, z_sems, label_sems, x_sems, c_sems):
     zs, xs, cs = sizes
     z, x, c = lax.axis_index("chan"), lax.axis_index("win"), lax.axis_index("grp")
 
@@ -175,8 +182,22 @@
     for d in range(1, zs):
         along_z[d] = send(mine_ref, own, z_sems, (d,), "chan", other(z, d))
     share(mine_ref, own, 0, 0, along_c)
-    keep = pltpu.make_async_copy(mine_ref, out_ref.at[own], own_sem)
+    told = []
+    for d in range(1, zs):
+        copy = pltpu.make_async_remote_copy(
+            src_ref=seen_ref,
+            dst_ref=labels_ref.at[z],
+            send_sem=label_sems.at[0, d],
+            recv_sem=label_sems.at[1, d],
+            device_id={"chan": other(z, d)},
+            device_id_type=pl.DeviceIdType.MESH,
+        )
+        copy.start()
+        told.append(copy)
+    keep = pltpu.make_async_copy(mine_ref, out_ref.at[own], own_sems.at[0])
     keep.start()
+    keep_labels = pltpu.make_async_copy(seen_ref, labels_ref.at[z], own_sems.at[1])
+    keep_labels.start()
 
     def relay_x(d):
         for e in range(1, xs):
@@ -196,13 +217,16 @@
     for copies in (along_z, along_x, along_c):
         for copy in copies.values():
             copy.wait_send()
+    for copy in told:
+        copy.wait()
     keep.wait()
-
-
-def select_kernel(wins, sources_ref, spectra_ref, chan_ref, src_ref):
+    keep_labels.wait()
+
+
+def select_kernel(sources_ref, labels_ref, spectra_ref, chan_ref, src_ref):
     blocks = spectra_ref.shape[0]
     cores = spectra_ref.shape[1]
-    count = spectra_ref.shape[2] - TAIL
+    count = spectra_ref.shape[2]
     channels = chan_ref.shape[0]
     groups, width = sources_ref.shape
     first = lax.axis_index("chan") * CH_DEV + lax.axis_index("win") * channels
@@ -215,13 +239,11 @@
     wanted = jnp.concatenate(wanted, axis=0)
     total = None
     for block in range(blocks):
-        digits = spectra_ref[block, 0, count : count + TAIL, : cores * count].astype(jnp.float32)
-        labels = (digits[0:1, :] * 64.0 + digits[1:2, :]).astype(jnp.int32)
-        pick = (wanted == labels).astype(jnp.float32).astype(jnp.bfloat16)
-        rows = jnp.concatenate([spectra_ref[block, c, :count, :] for c in range(cores)], axis=0)
+        pick = (wanted == labels_ref[block, :, : cores * count]).astype(jnp.float32).astype(jnp.bfloat16)
+        rows = jnp.concatenate([spectra_ref[block, c] for c in range(cores)], axis=0)
         part = dot(pick, rows)
         total = part if total is None else total + part
-    src_ref[...] = total[: groups * width]
+    src_ref[...] = total[: groups * width].astype(jnp.bfloat16)
     chan_ref[...] = total[groups * width :]
 
 
@@ -232,11 +254,12 @@
         for w in range(wins):
             at = w * 2 * FB
             p, q = src_ref[:, at : at + FB], src_ref[:, at + FB : at + 2 * FB]
-            a, b = chan_ref[c : c + 1, at : at + FB], chan_ref[c : c + 1, at + FB : at + 2 * FB]
+            row = chan_ref[c : c + 1, at : at + 2 * FB].astype(jnp.bfloat16)
+            a, b = row[:, :FB], row[:, FB:]
             re, im = a * p + b * q, b * p - a * q
             real = re if real is None else real + re
             imag = im if imag is None else imag + im
-        cross = jnp.concatenate([real.astype(jnp.bfloat16), imag.astype(jnp.bfloat16)], axis=1)
+        cross = jnp.concatenate([real, imag], axis=1)
         out_ref[c] = dot(cross, inverse)
 
 
@@ -253,7 +276,7 @@
     cores = lax.axis_size("grp")
     share = count // cores
     whole = lambda shape: pl.BlockSpec(shape, lambda i: (0,) * len(shape))
-    mine = pl.pallas_call(
+    mine, seen = pl.pallas_call(
         whiten_kernel,
         grid=(1,),
         in_specs=[
@@ -263,17 +286,19 @@
             whole((1, channel_list.shape[0])),
             pl.BlockSpec(memory_space=pl.ANY),
         ],
-        out_specs=whole((share + TAIL, 2 * FB)),
-        out_shape=jax.ShapeDtypeStruct((share + TAIL, 2 * FB), jnp.bfloat16),
+        out_specs=[whole((share, 2 * FB)), whole((1, 2 * FB))],
+        out_shape=[
+            jax.ShapeDtypeStruct((share, 2 * FB), jnp.bfloat16),
+            jax.ShapeDtypeStruct((1, 2 * FB), jnp.int32),
+        ],
         scratch_shapes=[
             pltpu.VMEM((share, L), jnp.bfloat16),
-            pltpu.VMEM((L, 2 * FB), jnp.bfloat16),
+            pltpu.VMEM((L // FOLD, 2 * FB), jnp.bfloat16),
             pltpu.VMEM((share, L), jnp.float32),
             pltpu.VMEM((share, L), jnp.bfloat16),
-            pltpu.VMEM((share, L), jnp.bfloat16),
+            pltpu.VMEM((FOLD * share, L // FOLD), jnp.bfloat16),
             pltpu.VMEM((384, 256), jnp.bfloat16),
             pltpu.VMEM((1, 256), jnp.float32),
-            pltpu.VMEM((1, 2 * FB), jnp.int32),
             pltpu.SemaphoreType.DMA,
         ],
         compiler_params=pltpu.CompilerParams(vmem_limit_bytes=VMEM_LIMIT),
@@ -286,29 +311,37 @@
         file_rows,
     )
 
-    block = (share + TAIL, 2 * FB)
+    block = (share, 2 * FB)
     gathered = (chan_count, wins, cores, *block)
     small = math.prod(gathered) * 2 <= 8 * 1024 * 1024
-    spectra = pl.pallas_call(
+    spectra, labels = pl.pallas_call(
         functools.partial(gather_kernel, (chan_count, wins, cores)),
-        in_specs=[pl.BlockSpec(memory_space=pltpu.VMEM)],
-        out_specs=pl.BlockSpec(memory_space=pltpu.VMEM if small else pl.ANY),
-        out_shape=jax.ShapeDtypeStruct(gathered, jnp.bfloat16),
+        in_specs=[pl.BlockSpec(memory_space=pltpu.VMEM)] * 2,
+        out_specs=[
+            pl.BlockSpec(memory_space=pltpu.VMEM if small else pl.ANY),
+            pl.BlockSpec(memory_space=pltpu.VMEM),
+        ],
+        out_shape=[
+            jax.ShapeDtypeStruct(gathered, jnp.bfloat16),
+            jax.ShapeDtypeStruct((chan_count, 1, 2 * FB), jnp.int32),
+        ],
         scratch_shapes=[
-            pltpu.SemaphoreType.DMA,
+            pltpu.SemaphoreType.DMA((2,)),
+            pltpu.SemaphoreType.DMA((2, chan_count)),
             pltpu.SemaphoreType.DMA((2, chan_count)),
             pltpu.SemaphoreType.DMA((2, chan_count, wins)),
             pltpu.SemaphoreType.DMA((2, chan_count, wins, cores)),
         ],
         compiler_params=pltpu.CompilerParams(collective_id=0, has_side_effects=True),
         name="gather",
-    )(mine)
+    )(mine, seen)
 
     chan_spec, src_spec = pl.pallas_call(
-        functools.partial(select_kernel, wins),
+        select_kernel,
         grid=(wins,),
         in_specs=[
             whole((groups, width)),
+            whole((chan_count, 1, 2 * FB)),
             pl.BlockSpec((chan_count, None, cores, *block), lambda w: (0, w, 0, 0, 0)),
         ],
         out_specs=[
@@ -317,11 +350,11 @@
         ],
         out_shape=[
             jax.ShapeDtypeStruct((channels, wins * 2 * FB), jnp.float32),
-            jax.ShapeDtypeStruct((sources, wins * 2 * FB), jnp.float32),
+            jax.ShapeDtypeStruct((sources, wins * 2 * FB), jnp.bfloat16),
         ],
         compiler_params=pltpu.CompilerParams(vmem_limit_bytes=VMEM_LIMIT),
         name="select",
-    )(source_channels, spectra)
+    )(source_channels, labels, spectra)
 
     step = 8
     return pl.pallas_call(

time: 38 us -> 34.4 us (0.905)
  Pallas kernels: 37.4 us -> 33.8 us
    pallas_call x1, Pallas kernels: 20.4 us -> 18.9 us  [local(): pl.pallas_call(functools.partial(gather_kernel, (chan_count, wins, cores)...]
    pallas_call x1, Pallas kernels: 5.66 us -> 4.4 us  [local(): pl.pallas_call(whiten_kernel, grid=(1,), in_specs=[whole((1, TAPS)), whol...]
    pallas_call x1, Pallas kernels: 8.48 us -> 7.75 us  [local(): pl.pallas_call(functools.partial(correlate_kernel, wins), grid=(channels...]
where the time goes in v2:
time: 34.4 us; the launch traced here: 33.8 us
  Pallas kernels  33.8 us (98%)
    pallas_call x1, Pallas kernels, local(): pl.pallas_call(functools.partial(gather_kernel, (chan_count, wins, cores)...  18.9 us
    pallas_call x1, Pallas kernels, local(): pl.pallas_call(functools.partial(correlate_kernel, wins), grid=(channels...  7.75 us
    pallas_call x1, Pallas kernels, local(): pl.pallas_call(whiten_kernel, grid=(1,), in_specs=[whole((1, TAPS)), whol...  4.4 us
    pallas_call x1, Pallas kernels, local(): pl.pallas_call(select_kernel, grid=(wins,), in_specs=[whole((groups, widt...  2.79 us

profile of v2, /device:TPU:0, one launch (start us, length us, event | category | flops | bytes accessed | tf_op | source)
XLA Modules:
  0.0 33.8 jit_solution(16210738833240155491)
XLA Ops:
  0.0 4.4 %whiten.1 = (bf16[64,512]{1,0:T(8,128)(2,1)}, s32[1,512]{1,0:T(1,128)}) custom-call(bf16[1,64]{1,0:T(2,128)(2,1)} %bitcast.3, f32[64,512]{1,0:T(8,128)} %constant.6.clone.coarse_ref, f32[64,512]{1,0:T(8,128)} %constant.7.clone.fine_ref, s32[1,160]{1,0:T(1,128)} %bitcast.2, bf16[160,4096]{1,0:T(8,128)(2,1)} %file_ref.1), custom_call_target="tpu_custom_call" | custom-call | tf_op jit(solution)/shard_map/whiten/pallas_call | solution.py:279
  4.4 18.9 %gather.1 = (bf16[4,2,2,64,512]{4,3,2,1,0:T(8,128)(2,1)}, s32[4,1,512]{2,1,0:T(1,128)}) custom-call(bf16[64,512]{1,0:T(8,128)(2,1)} %get-tuple-element.11.mine_ref, s32[1,512]{1,0:T(1,128)} %get-tuple-element.12.seen_ref), custom_call_target="tpu_custom_call" | custom-call | tf_op jit(solution)/shard_map/gather/pallas_call | solution.py:317
  23.3 2.8 %select.1 = (f32[64,1024]{1,0:T(8,128)}, bf16[128,1024]{1,0:T(8,128)(2,1)}) custom-call(s32[2,64]{1,0:T(2,128)} %sources_ref.1, s32[4,1,512]{2,1,0:T(1,128)} %get-tuple-element.13.labels_ref, bf16[4,2,2,64,512]{4,3,2,1,0:T(8,128)(2,1)} %get-tuple-element.14.spectra_ref), custom_call_target="tpu_custom_call" | custom-call | tf_op jit(solution)/shard_map/select/pallas_call | solution.py:339
  26.1 7.8 %correlate.1 = f32[64,128,256]{2,1,0:T(8,128)} custom-call(bf16[512,256]{1,0:T(8,128)(2,1)} %constant.8.clone.inverse_ref, bf16[128,1024]{1,0:T(8,128)(2,1)} %get-tuple-element.15.src_ref, f32[64,1024]{1,0:T(8,128)} %get-tuple-element.16.chan_ref), custom_call_target="tpu_custom_call" | custom-call | tf_op jit(solution)/shard_map/correlate/pallas_call | solution.py:360
